TPU v7x, 32 devices: a whole 2x2x4 slice. The times are simulated.
32 devices in a mesh: wide: 16 (over z, y, core), narrow: 2 (over x).
Axes of the slice: x: 2, y: 2, z: 4, core: 2. Of those that a mesh axis runs over, the one named last changes fastest.
Arguments:
- block_in: bfloat16 [32768, 768], P(('wide', 'narrow')), may hold values from -6 to 6
- out_grad: bfloat16 [32768, 768], P(('wide', 'narrow')), may hold values from -6 to 6
- seq_lens: int32 [16, 4], P('wide'), may hold values from 0 to 2048, as said below
- qkv_weight: bfloat16 [768, 2304], P(None, 'narrow'), may hold values from -0.21875 to 0.21875
- qkv_bias: bfloat16 [2304], P('narrow'), may hold values from -0.5 to 0.5
- out_weight: bfloat16 [768, 768], P('narrow'), may hold values from -0.875 to 0.875
- out_bias: bfloat16 [768], replicated, may hold values from -0.5 to 0.5
- up_weight: bfloat16 [768, 3072], P(None, 'narrow'), may hold values from -0.21875 to 0.21875
- up_bias: bfloat16 [3072], P('narrow'), may hold values from -0.5 to 0.5
- down_weight: bfloat16 [3072, 768], P('narrow'), may hold values from -0.109375 to 0.109375
- down_bias: bfloat16 [768], replicated, may hold values from -0.5 to 0.5
- attn_gain: bfloat16 [768], replicated, may hold values from 0.5 to 1.5
- attn_shift: bfloat16 [768], replicated, may hold values from -0.5 to 0.5
- ffn_gain: bfloat16 [768], replicated, may hold values from 0.5 to 1.5
- ffn_shift: bfloat16 [768], replicated, may hold values from -0.5 to 0.5
Outputs:
- block_out: bfloat16 [32768, 768], P(('wide', 'narrow'))
- in_grad: bfloat16 [32768, 768], P(('wide', 'narrow'))
- grad_qkv_weight: float32 [768, 2304], P(None, 'narrow')
- grad_qkv_bias: float32 [2304], P('narrow')
- grad_out_weight: float32 [768, 768], P('narrow')
- grad_out_bias: float32 [768], replicated
- grad_up_weight: float32 [768, 3072], P(None, 'narrow')
- grad_up_bias: float32 [3072], P('narrow')
- grad_down_weight: float32 [3072, 768], P('narrow')
- grad_down_bias: float32 [768], replicated
- grad_attn_gain: float32 [768], replicated
- grad_attn_shift: float32 [768], replicated
- grad_ffn_gain: float32 [768], replicated
- grad_ffn_shift: float32 [768], replicated
Inputs may be any that keep to these rules, and one draw needn't show every extreme that they name: `seq_lens`: each row is either 2048 followed by zeros or 512 in every slot; both kinds occur in every draw.
All inputs are finite; a program needn't handle non-finite values.
Results may differ from a plain program's by a relative error of at most 0.011.
Values may be sent and summed in bfloat16 or wider, within the bound.
No kernel may reach another device: no remote copies, remote signals or barrier semaphores. Data moves between devices by JAX's collectives and lax.ppermute only.
A program may use at most 256 MiB of HBM per device.

v0:
```python
import jax
import jax.numpy as jnp
from jax import lax
from jax.sharding import PartitionSpec as P

HD = 64
ROT = 16
EPS = 1e-05
NEG = -1e30
SCALE = 0.125


def norm_stats(rows):
    rows = rows.astype(jnp.float32)
    center = jnp.mean(rows, axis=-1, keepdims=True)
    offset = rows - center
    spread = jnp.mean(offset * offset, axis=-1, keepdims=True)
    inverse = lax.rsqrt(spread + EPS)
    return (offset * inverse, inverse)


def norm_back(grad_rows, normed, inverse, gain):
    scaled = grad_rows * gain.astype(jnp.float32)
    return inverse * (
        scaled
        - jnp.mean(scaled, axis=-1, keepdims=True)
        - normed * jnp.mean(scaled * normed, axis=-1, keepdims=True)
    )


def rotate(heads_rows, place, direction):
    half = ROT // 2
    freq = 1.0 / 10000.0 ** (jnp.arange(half, dtype=jnp.float32) * 2.0 / ROT)
    angle = place[:, None].astype(jnp.float32) * freq[None, :]
    cosine = jnp.cos(angle)[:, None, :]
    sine = jnp.sin(angle)[:, None, :] * direction
    first = heads_rows[..., :half]
    second = heads_rows[..., half:ROT]
    return jnp.concatenate(
        [first * cosine - second * sine, second * cosine + first * sine, heads_rows[..., ROT:]],
        axis=-1,
    )


def positions(lens_row, group_rows):
    ends = jnp.cumsum(lens_row)
    starts = ends - lens_row
    token_index = jnp.arange(group_rows, dtype=jnp.int32)
    segment = jnp.sum((token_index[:, None] >= ends[None, :]).astype(jnp.int32), axis=1)
    chosen = segment[:, None] == jnp.arange(lens_row.shape[0], dtype=jnp.int32)[None, :]
    begin = jnp.sum(jnp.where(chosen, starts[None, :], 0), axis=1)
    return (segment, token_index - begin)


def contract_rows(left, right):
    return lax.dot_general(
        left, right, (((0,), (0,)), ((), ())), preferred_element_type=jnp.float32
    )


def contract_cols(left, right):
    return lax.dot_general(
        left, right, (((1,), (1,)), ((), ())), preferred_element_type=jnp.float32
    )


def block_scores(query_rows, key_rows, segment, row_start):
    row_count = query_rows.shape[0]
    key_count = key_rows.shape[0]
    raw = (
        jnp.einsum("qhd,khd->hqk", query_rows, key_rows, preferred_element_type=jnp.float32) * SCALE
    )
    query_index = row_start + jnp.arange(row_count, dtype=jnp.int32)
    key_index = jnp.arange(key_count, dtype=jnp.int32)
    allowed = (
        segment[row_start : row_start + row_count][:, None] == segment[:key_count][None, :]
    ) & (key_index[None, :] <= query_index[:, None])
    return jnp.where(allowed[None], raw, NEG)


def per_device(
    block_in,
    out_grad,
    seq_lens,
    qkv_weight,
    qkv_bias,
    out_weight,
    out_bias,
    up_weight,
    up_bias,
    down_weight,
    down_bias,
    attn_gain,
    attn_shift,
    ffn_gain,
    ffn_shift,
):
    gathered = lax.all_gather(block_in, "narrow", axis=0, tiled=True)
    group_rows = gathered.shape[0]
    local_heads = qkv_weight.shape[1] // (3 * HD)
    segment, place = positions(seq_lens[0], group_rows)
    normed, inverse = norm_stats(gathered)
    first_in = (normed * attn_gain.astype(jnp.float32) + attn_shift.astype(jnp.float32)).astype(
        jnp.bfloat16
    )
    second_in = (normed * ffn_gain.astype(jnp.float32) + ffn_shift.astype(jnp.float32)).astype(
        jnp.bfloat16
    )
    packed = (
        jnp.dot(first_in, qkv_weight, preferred_element_type=jnp.float32)
        + qkv_bias.astype(jnp.float32)
    ).reshape(group_rows, local_heads, 3 * HD)
    queries = rotate(packed[..., :HD], place, 1.0).astype(jnp.bfloat16)
    keys_all = rotate(packed[..., HD : 2 * HD], place, 1.0).astype(jnp.bfloat16)
    values = packed[..., 2 * HD :].astype(jnp.bfloat16)
    hidden_pre = jnp.dot(second_in, up_weight, preferred_element_type=jnp.float32) + up_bias.astype(
        jnp.float32
    )
    activated = jax.nn.gelu(hidden_pre, approximate=False).astype(jnp.bfloat16)
    block_rows = min(512, group_rows)
    context_parts = []
    total_parts = []
    for row_start in range(0, group_rows, block_rows):
        row_stop = row_start + block_rows
        scores = block_scores(queries[row_start:row_stop], keys_all[:row_stop], segment, row_start)
        top = jnp.max(scores, axis=-1, keepdims=True)
        expo = jnp.exp(scores - top)
        row_total = jnp.sum(expo, axis=-1, keepdims=True)
        attn_probs = expo / row_total
        total_parts.append(top + jnp.log(row_total))
        context_parts.append(
            jnp.einsum(
                "hqk,khd->qhd",
                attn_probs.astype(jnp.bfloat16),
                values[:row_stop],
                preferred_element_type=jnp.float32,
            )
        )
    context = (
        jnp.concatenate(context_parts, axis=0)
        .reshape(group_rows, local_heads * HD)
        .astype(jnp.bfloat16)
    )
    partial_out = jnp.dot(context, out_weight, preferred_element_type=jnp.float32) + jnp.dot(
        activated, down_weight, preferred_element_type=jnp.float32
    )
    summed = lax.psum_scatter(partial_out, "narrow", scatter_dimension=0, tiled=True)
    block_out = (
        block_in.astype(jnp.float32)
        + summed
        + out_bias.astype(jnp.float32)
        + down_bias.astype(jnp.float32)
    ).astype(jnp.bfloat16)
    grad_rows = lax.all_gather(out_grad, "narrow", axis=0, tiled=True)
    bias_grad = jnp.sum(out_grad.astype(jnp.float32), axis=0)
    grad_out_w = contract_rows(context, grad_rows)
    grad_context = (
        contract_cols(grad_rows, out_weight)
        .astype(jnp.bfloat16)
        .reshape(group_rows, local_heads, HD)
    )
    grad_down_w = contract_rows(activated, grad_rows)
    grad_act = contract_cols(grad_rows, down_weight)
    _, gelu_back = jax.vjp(lambda value: jax.nn.gelu(value, approximate=False), hidden_pre)
    grad_hidden = gelu_back(grad_act)[0].astype(jnp.bfloat16)
    grad_up_w = contract_rows(second_in, grad_hidden)
    grad_up_b = jnp.sum(grad_hidden.astype(jnp.float32), axis=0)
    grad_second = contract_cols(grad_hidden, up_weight)
    query_parts = []
    grad_keys = jnp.zeros((group_rows, local_heads, HD), jnp.float32)
    grad_values = jnp.zeros((group_rows, local_heads, HD), jnp.float32)
    for part_index, row_start in enumerate(range(0, group_rows, block_rows)):
        row_stop = row_start + block_rows
        scores = block_scores(queries[row_start:row_stop], keys_all[:row_stop], segment, row_start)
        attn_probs = jnp.exp(scores - total_parts[part_index])
        grad_block = grad_context[row_start:row_stop]
        grad_values = grad_values.at[:row_stop].add(
            jnp.einsum(
                "hqk,qhd->khd",
                attn_probs.astype(jnp.bfloat16),
                grad_block,
                preferred_element_type=jnp.float32,
            )
        )
        grad_probs = jnp.einsum(
            "qhd,khd->hqk", grad_block, values[:row_stop], preferred_element_type=jnp.float32
        )
        weighted = jnp.sum(attn_probs * grad_probs, axis=-1, keepdims=True)
        grad_scores = (attn_probs * (grad_probs - weighted)).astype(jnp.bfloat16)
        query_parts.append(
            jnp.einsum(
                "hqk,khd->qhd", grad_scores, keys_all[:row_stop], preferred_element_type=jnp.float32
            )
            * SCALE
        )
        grad_keys = grad_keys.at[:row_stop].add(
            jnp.einsum(
                "hqk,qhd->khd",
                grad_scores,
                queries[row_start:row_stop],
                preferred_element_type=jnp.float32,
            )
            * SCALE
        )
    grad_queries = rotate(jnp.concatenate(query_parts, axis=0), place, -1.0)
    grad_keys = rotate(grad_keys, place, -1.0)
    grad_packed = (
        jnp.concatenate([grad_queries, grad_keys, grad_values], axis=-1)
        .reshape(group_rows, local_heads * 3 * HD)
        .astype(jnp.bfloat16)
    )
    grad_qkv_w = contract_rows(first_in, grad_packed)
    grad_qkv_b = jnp.sum(grad_packed.astype(jnp.float32), axis=0)
    grad_first = contract_cols(grad_packed, qkv_weight)
    grad_qkv_w, grad_qkv_b, grad_out_w, grad_up_w, grad_up_b, grad_down_w = lax.psum(
        (grad_qkv_w, grad_qkv_b, grad_out_w, grad_up_w, grad_up_b, grad_down_w), "wide"
    )
    first_share, second_share = (
        lax.psum_scatter(grad_first, "narrow", scatter_dimension=0, tiled=True),
        lax.psum_scatter(grad_second, "narrow", scatter_dimension=0, tiled=True),
    )
    own_normed, own_inverse = norm_stats(block_in)
    in_grad = (
        out_grad.astype(jnp.float32)
        + norm_back(first_share, own_normed, own_inverse, attn_gain)
        + norm_back(second_share, own_normed, own_inverse, ffn_gain)
    )
    vectors = (
        jnp.sum(first_share * own_normed, axis=0),
        jnp.sum(first_share, axis=0),
        jnp.sum(second_share * own_normed, axis=0),
        jnp.sum(second_share, axis=0),
        bias_grad,
    )
    attn_gain_g, attn_shift_g, ffn_gain_g, ffn_shift_g, bias_total = lax.psum(
        (vectors[0], vectors[1], vectors[2], vectors[3], vectors[4]), ("wide", "narrow")
    )
    return (
        block_out,
        in_grad.astype(jnp.bfloat16),
        grad_qkv_w,
        grad_qkv_b,
        grad_out_w,
        bias_total,
        grad_up_w,
        grad_up_b,
        grad_down_w,
        bias_total,
        attn_gain_g,
        attn_shift_g,
        ffn_gain_g,
        ffn_shift_g,
    )


def solution(mesh):
    placed = (
        P(("wide", "narrow"), None),
        P(("wide", "narrow"), None),
        P("wide", None),
        P(None, "narrow"),
        P("narrow"),
        P("narrow", None),
        P(),
        P(None, "narrow"),
        P("narrow"),
        P("narrow", None),
        P(),
        P(),
        P(),
        P(),
        P(),
    )
    return jax.shard_map(
        per_device,
        mesh=mesh,
        in_specs=placed,
        out_specs=(
            P(("wide", "narrow"), None),
            P(("wide", "narrow"), None),
            P(None, "narrow"),
            P("narrow"),
            P("narrow", None),
            P(),
            P(None, "narrow"),
            P("narrow"),
            P("narrow", None),
            P(),
            P(),
            P(),
            P(),
            P(),
        ),
        check_vma=False,
    )
```

profile of v0, /device:TPU:0, one launch (start us, length us, event | category | flops | bytes accessed | tf_op | source)
XLA Modules:
  0.0 851.6 jit_solution(16737983099656652931)
XLA Ops:
  19.7 37.6 %all-gather.3.cloned.1.call-done = bf16[2048,768]{1,0:T(8,128)(2,1)} async-done(((bf16[1024,768]{1,0:T(8,128)(2,1)}), bf16[2048,768]{1,0:T(8,128)(2,1)}) %all-gather.3.cloned.1.call-update) | async-done | bytes 3145744 | tf_op jit(solution)/shard_map/all_gather | solution.py:98
  62.6 41.1 %all-gather.5.cloned.1.call-done = bf16[2048,768]{1,0:T(8,128)(2,1)} async-done(((bf16[1024,768]{1,0:T(8,128)(2,1)}), bf16[2048,768]{1,0:T(8,128)(2,1)}) %all-gather.5.cloned.1.call-update) | async-done | bytes 3145744 | tf_op jit(solution)/shard_map/all_gather | solution.py:154
  145.3 8.0 multiply_reduce_fusion.2
  168.1 8.3 fusion.142
  176.4 9.6 %fusion.2 = f32[6,512]{1,0:T(8,128)} fusion(f32[6,512,1536]{2,1,0:T(8,128)} %get-tuple-element.179, f32[6,512]{1,0:T(8,128)S(1)} %get-tuple-element.178), kind=kLoop, calls=%fused_computation.15 | loop fusion | flops 9434112 | bytes 18898944 | tf_op jit(solution)/shard_map/reduce_sum | solution.py:128
  186.8 13.2 %multiply_reduce_fusion.1 = (f32[6,512]{1,0:T(8,128)S(1)}, f32[6,512,1536]{2,1,0:T(8,128)}) fusion(f32[6,512,1536]{2,1,0:T(8,128)} %get-tuple-element.179, f32[6,512]{1,0:T(8,128)S(1)} %log_add_fusion.1, bf16[512,6,64]{0,2,1:T(8,128)(2,1)} %bitcast.112, bf16[2048,6,192]{0,2,1:T(8,128)(2,1)} %copy-done.11), kind=kOutput, calls=%fused_computation.10 | convolution fusion | flops 618132480 | bytes 39346176 | tf_op jit(solution)/shard_map/qhd,khd->hqk/dot_general | solution.py:185
  200.0 8.1 fusion.75
  209.7 13.0 %multiply_convert_fusion.1 = bf16[6,512,1536]{2,1,0:T(8,128)(2,1)S(1)} fusion(f32[6,512,1536]{2,1,0:T(8,128)} %get-tuple-element.181, f32[6,512,1536]{2,1,0:T(8,128)} %get-tuple-element.179, f32[6,512]{1,0:T(8,128)S(1)} %get-tuple-element.180, f32[6,512]{1,0:T(8,128)S(1)} %log_add_fusion.1), kind=kLoop, calls=%fused_computation.9 | loop fusion | flops 18874368 | bytes 47210496 | tf_op jit(solution)/shard_map/convert_element_type | solution.py:189
  228.5 10.7 %fusion.141 = (f32[6,512]{1,0:T(8,128)S(1)}, f32[6,512,2048]{2,1,0:T(8,128)}) fusion(bf16[2048,6,48]{0,2,1:T(8,128)(2,1)S(1)} %get-tuple-element.158, bf16[2048,6,8]{0,2,1:T(8,128)(2,1)S(1)} %copy-done.33, bf16[2048,6,8]{0,2,1:T(8,128)(2,1)S(1)} %copy-done.30, bf16[2048,6,64]{0,2,1:T(8,128)(2,1)S(1)} %copy-done.16, pred[512,2048]{1,0:T(8,128)(4,1)S(1)} %copy-done.42), kind=kOutput, calls=%fused_computation.222 | convolution fusion | flops 828896256 | bytes 28192768 | tf_op jit(solution)/shard_map/qhd,khd->hqk/dot_general | solution.py:71
  239.2 10.4 %fusion = f32[6,512]{1,0:T(8,128)S(1)} fusion(f32[6,512,2048]{2,1,0:T(8,128)} %get-tuple-element.175, f32[6,512]{1,0:T(8,128)S(1)} %get-tuple-element.174), kind=kLoop, calls=%fused_computation.6 | loop fusion | flops 12579840 | bytes 25190400 | tf_op jit(solution)/shard_map/reduce_sum | solution.py:128
  250.2 17.0 %multiply_reduce_fusion = (f32[6,512]{1,0:T(8,128)}, f32[6,512,2048]{2,1,0:T(8,128)}) fusion(f32[6,512,2048]{2,1,0:T(8,128)} %get-tuple-element.175, f32[6,512]{1,0:T(8,128)S(1)} %log_add_fusion, bf16[512,6,64]{0,2,1:T(8,128)(2,1)} %bitcast.110, bf16[2048,6,192]{0,2,1:T(8,128)(2,1)} %copy-done.11), kind=kOutput, calls=%fused_computation.1 | convolution fusion | flops 824177664 | bytes 52322304 | tf_op jit(solution)/shard_map/qhd,khd->hqk/dot_general | solution.py:185
  267.2 21.6 %multiply_convert_fusion = bf16[6,512,2048]{2,1,0:T(8,128)(2,1)} fusion(f32[6,512,2048]{2,1,0:T(8,128)} %get-tuple-element.177, f32[6,512,2048]{2,1,0:T(8,128)} %get-tuple-element.175, f32[6,512]{1,0:T(8,128)} %get-tuple-element.176, f32[6,512]{1,0:T(8,128)S(1)} %log_add_fusion), kind=kLoop, calls=%fused_computation | loop fusion | flops 25165824 | bytes 62939136 | tf_op jit(solution)/shard_map/convert_element_type | solution.py:189
  288.9 8.7 %fusion.91 = f32[512,6,64]{0,2,1:T(8,128)S(1)} fusion(bf16[6,512,2048]{2,1,0:T(8,128)(2,1)} %multiply_convert_fusion, bf16[2048,6,48]{0,2,1:T(8,128)(2,1)S(1)} %get-tuple-element.158, bf16[2048,6,8]{0,2,1:T(8,128)(2,1)S(1)} %copy-done.34, bf16[2048,6,8]{0,2,1:T(8,128)(2,1)S(1)} %copy-done.31), kind=kOutput, calls=%fused_computation.141 | convolution fusion | flops 810221568 | bytes 14942208 | tf_op jit(solution)/shard_map/hqk,khd->qhd/dot_general | solution.py:191
  310.1 12.0 %fusion.60 = bf16[2048,6,192]{0,2,1:T(8,128)(2,1)} fusion(bf16[2048,6,192]{0,2,1:T(8,128)(2,1)} %slice_dynamic-update-slice_fusion, f32[2048,6,64]{0,2,1:T(8,128)S(1)} %copy-done.10, bf16[512,6,64]{0,2,1:T(8,128)(2,1)S(1)} %bitcast.111, f32[6,512,2048]{2,1,0:T(8,128)} %get-tuple-element.175, f32[6,512]{1,0:T(8,128)S(1)} %log_add_fusion), kind=kOutput, calls=%fused_computation.104 | convolution fusion | flops 818675712 | bytes 31862784 | tf_op jit(solution)/shard_map/hqk,qhd->khd/dot_general | solution.py:178
  322.1 9.0 %fusion.146 = f32[2048,768]{1,0:T(8,128)} fusion(bf16[2048,1152]{0,1:T(8,128)(2,1)} %bitcast.26, bf16[768,1152]{1,0:T(8,128)(2,1)S(1)} %copy-done.84), kind=kOutput, calls=%fused_computation.227 | convolution fusion | flops 3623878656 | bytes 12779520 | tf_op jit(solution)/shard_map/dot_general | solution.py:62
  331.8 35.4 %multiply_convert_fusion.3 = (bf16[2048,1536]{1,0:T(8,128)(2,1)}, f32[2048,1536]{1,0:T(8,128)}, f32[2048,1536]{1,0:T(8,128)}) fusion(f32[1536]{0:T(1024)S(1)} %convert_element_type.145, bf16[768,1536]{1,0:T(8,128)(2,1)S(1)} %copy-done, bf16[2048,768]{1,0:T(8,128)(2,1)} %all-gather.3.cloned.1.call-done, f32[768]{0:T(1024)S(1)} %convert_element_type.143, ...), kind=kOutput, calls=%fused_computation.25 | convolution fusion | flops 5048893440 | bytes 36990976 | tf_op jit(solution)/shard_map/dot_general | solution.py:116
  367.2 16.0 %convert_reduce_fusion = (f32[1536]{0:T(1024)S(1)}, bf16[2048,1536]{1,0:T(8,128)(2,1)}) fusion(f32[2048,1536]{1,0:T(8,128)} %get-tuple-element.153, bf16[2048,768]{1,0:T(8,128)(2,1)S(1)} %copy-done.79, bf16[1536,768]{1,0:T(8,128)(2,1)S(1)} %copy-done.81, f32[2048,1536]{1,0:T(8,128)} %get-tuple-element.190, f32[1536]{0:T(1024)S(1)} %convert_element_type.145), kind=kOutput, calls=%fused_computation.19 | convolution fusion | flops 4885314048 | bytes 36974592 | tf_op jit(solution)/shard_map/dot_general | solution.py:62
  383.2 9.7 %fusion.147 = f32[2048,768]{1,0:T(8,128)} fusion(bf16[2048,1536]{1,0:T(8,128)(2,1)} %get-tuple-element.192, bf16[768,1536]{1,0:T(8,128)(2,1)S(1)} %copy-done), kind=kOutput, calls=%fused_computation.228 | convolution fusion | flops 4831838208 | bytes 14942208 | tf_op jit(solution)/shard_map/dot_general | solution.py:62
  411.8 12.2 %fusion.101 = bf16[512,6,64]{0,2,1:T(8,128)(2,1)S(1)} fusion(f32[6,512,2048]{2,1,0:T(8,128)} %get-tuple-element.175, f32[6,512]{1,0:T(8,128)S(1)} %copy-done.60, f32[6,512]{1,0:T(8,128)S(1)} %copy-done.58, bf16[2048,6,192]{0,2,1:T(8,128)(2,1)} %copy-done.11), kind=kOutput, calls=%fused_computation.152 | convolution fusion | flops 824377344 | bytes 27156480 | tf_op jit(solution)/shard_map/hqk,khd->qhd/dot_general | solution.py:132
  441.7 9.7 %fusion.134 = f32[768,1152]{1,0:T(8,128)} fusion(bf16[2048,1152]{0,1:T(8,128)(2,1)} %bitcast.26, bf16[2048,768]{1,0:T(8,128)(2,1)S(1)} %copy-done.18, f32[768]{0:T(1024)S(1)} %copy-done.71, f32[768]{0:T(1024)S(1)} %copy-done.62, f32[2048]{0:T(1024)S(1)} %copy-done.68, f32[2048]{0:T(1024)S(1)} %copy-done.66), kind=kOutput, calls=%fused_computation.218 | convolution fusion | flops 3633315840 | bytes 11425792 | tf_op jit(solution)/shard_map/dot_general | solution.py:56
  473.5 61.1 %all-reduce.3 = (f32[1152]{0:T(1024)}, f32[1536]{0:T(1024)}) all-reduce(f32[1152]{0:T(1024)S(1)} %reduce_sum.246, f32[1536]{0:T(1024)S(1)} %get-tuple-element.191), channel_id=1, replica_groups=mesh['wide'=16,'narrow'=2] {'wide'}, use_global_device_ids=true, to_apply=%region_28.29 | all-reduce | flops 2688 | bytes 21504 | tf_op jit(solution)/shard_map/psum | solution.py:215
  539.3 27.6 %reduce-scatter.4.cloned.1.call-done = f32[1024,768]{1,0:T(8,128)} async-done(((f32[2048,768]{1,0:T(8,128)}), f32[1024,768]{1,0:T(8,128)}) %reduce-scatter.4.cloned.1.call-update) | async-done | bytes 3145744 | tf_op jit(solution)/shard_map/reduce_scatter | solution.py:147
  573.8 41.8 %all-reduce.2 = (f32[768]{0:T(1024)S(1)}, f32[768]{0:T(1024)}, f32[768]{0:T(1024)}, f32[768]{0:T(1024)}, f32[768]{0:T(1024)}) all-reduce(f32[768]{0:T(1024)S(1)} %get-tuple-element.160, f32[768]{0:T(1024)S(1)} %get-tuple-element.128, f32[768]{0:T(1024)S(1)} %get-tuple-element.133, ...), channel_id=1, replica_groups=mesh['wide'=16,'narrow'=2] {'wide','narrow'}, use_global_device_ids=true, to_apply=%region_31.32 | all-reduce | flops 3840 | bytes 30720 | tf_op jit(solution)/shard_map/psum | solution.py:235
  615.6 217.2 %all-reduce.7.cloned.1.call-done = (f32[768,1152]{1,0:T(8,128)}, f32[384,768]{1,0:T(8,128)}, f32[768,1536]{1,0:T(8,128)}, f32[1536,768]{1,0:T(8,128)}) async-done(((f32[768,1152]{1,0:T(8,128)}, f32[384,768]{1,0:T(8,128)}, f32[768,1536]{1,0:T(8,128)}, f32[1536,768]{1,0:T(8,128)}), (f32[768,1152]{1,0:T(8,128)}, f32[384,768]{1,0:T(8,128)}, f32[768,1536]{1,0:T(8,128)}, ...) | async-done | bytes 14155792 | tf_op jit(solution)/shard_map/psum | solution.py:215
  (304 shorter events, 177.0 us)
Async XLA Ops:
  7.2 324.6 %copy-start = (bf16[768,1536]{1,0:T(8,128)(2,1)S(1)}, bf16[768,1536]{1,0:T(8,128)(2,1)}, u32[]{:S(2)}) copy-start(bf16[768,1536]{1,0:T(8,128)(2,1)} %param.42) | copy-start | bytes 7077892
  7.2 96.6 %copy-start.43 = (bf16[384,768]{1,0:T(8,128)(2,1)S(1)}, bf16[384,768]{1,0:T(8,128)(2,1)}, u32[]{:S(2)}) copy-start(bf16[384,768]{1,0:T(8,128)(2,1)} %param.40) | copy-start | bytes 1769476
  7.2 50.0 %all-gather.3.cloned.1.call-start = ((), (), s32[]{:S(2)}) async-start(), calls=%async_computation.3 | async-start | bytes 4718592 | tf_op jit(solution)/shard_map/all_gather | solution.py:98
  7.9 95.8 %all-gather.5.cloned.1.call-start = ((), (), s32[]{:S(2)}) async-start(), calls=%async_computation.5 | async-start | bytes 4718592 | tf_op jit(solution)/shard_map/all_gather | solution.py:154
  8.7 525.9 %reduce-scatter.6.cloned.1.call-start = ((), (), s32[]{:S(2)}) async-start(), calls=%async_computation.6 | async-start | bytes 9437184 | tf_op jit(solution)/shard_map/reduce_scatter | solution.py:219
  10.9 97.4 %copy-start.61 = (f32[768]{0:T(1024)}, f32[768]{0:T(1024)S(1)}, u32[]{:S(2)}) copy-start(f32[768]{0:T(1024)S(1)} %convert_element_type.131) | copy-start | bytes 9220
  11.6 96.8 %copy-start.70 = (f32[768]{0:T(1024)}, f32[768]{0:T(1024)S(1)}, u32[]{:S(2)}) copy-start(f32[768]{0:T(1024)S(1)} %convert_element_type.132) | copy-start | bytes 9220
  59.6 48.8 %copy-start.65 = (f32[2048]{0:T(1024)}, f32[2048]{0:T(1024)S(1)}, u32[]{:S(2)}) copy-start(f32[2048]{0:T(1024)S(1)} %broadcast_multiply_fusion.1) | copy-start | bytes 24580
  62.6 45.8 %copy-start.67 = (f32[2048]{0:T(1024)}, f32[2048]{0:T(1024)S(1)}, u32[]{:S(2)}) copy-start(f32[2048]{0:T(1024)S(1)} %add_rsqrt_fusion) | copy-start | bytes 24580
  123.5 44.6 %copy-start.12 = (bf16[2048,6,64]{0,2,1:T(8,128)(2,1)}, bf16[2048,6,64]{0,2,1:T(8,128)(2,1)S(1)}, u32[]{:S(2)}) copy-start(bf16[2048,6,64]{0,2,1:T(8,128)(2,1)S(1)} %get-tuple-element.194) | copy-start | bytes 4718596
  142.3 15.2 %copy-start.1 = (f32[6,512,1024]{2,1,0:T(8,128)}, f32[6,512,1024]{2,1,0:T(8,128)S(1)}, u32[]{:S(2)}) copy-start(f32[6,512,1024]{2,1,0:T(8,128)S(1)} %get-tuple-element.183) | copy-start | bytes 37748740
  267.2 21.6 %copy-start.31 = (bf16[2048,6,8]{0,2,1:T(8,128)(2,1)S(1)}, bf16[2048,6,8]{0,2,1:T(8,128)(2,1)}, u32[]{:S(2)}) copy-start(bf16[2048,6,8]{0,2,1:T(8,128)(2,1)} %copy-done.29) | copy-start | bytes 589828
  267.2 21.6 %copy-start.34 = (bf16[2048,6,8]{0,2,1:T(8,128)(2,1)S(1)}, bf16[2048,6,8]{0,2,1:T(8,128)(2,1)}, u32[]{:S(2)}) copy-start(bf16[2048,6,8]{0,2,1:T(8,128)(2,1)} %copy-done.32) | copy-start | bytes 589828
  331.1 203.5 %reduce-scatter.8.cloned.1.call-start = ((), (), s32[]{:S(2)}) async-start(), calls=%async_computation.7 | async-start | bytes 9437184 | tf_op jit(solution)/shard_map/reduce_scatter | solution.py:220
  331.7 35.4 %copy-start.63 = (f32[768]{0:T(1024)}, f32[768]{0:T(1024)S(1)}, u32[]{:S(2)}) copy-start(f32[768]{0:T(1024)S(1)} %convert_element_type.142) | copy-start | bytes 9220
  331.7 35.4 %copy-start.72 = (f32[768]{0:T(1024)}, f32[768]{0:T(1024)S(1)}, u32[]{:S(2)}) copy-start(f32[768]{0:T(1024)S(1)} %convert_element_type.143) | copy-start | bytes 9220
  331.8 35.4 %copy-start.79 = (bf16[2048,768]{1,0:T(8,128)(2,1)S(1)}, bf16[2048,768]{1,0:T(8,128)(2,1)}, u32[]{:S(2)}) copy-start(bf16[2048,768]{1,0:T(8,128)(2,1)} %all-gather.5.cloned.1.call-done) | copy-start | bytes 9437188
  331.8 35.4 %copy-start.81 = (bf16[1536,768]{1,0:T(8,128)(2,1)S(1)}, bf16[1536,768]{1,0:T(8,128)(2,1)}, u32[]{:S(2)}) copy-start(bf16[1536,768]{1,0:T(8,128)(2,1)} %param.44) | copy-start | bytes 7077892
  393.0 173.8 %reduce-scatter.4.cloned.1.call-start = ((), (), s32[]{:S(2)}) async-start(), calls=%async_computation.4 | async-start | bytes 9437184 | tf_op jit(solution)/shard_map/reduce_scatter | solution.py:147
  436.4 396.4 %all-reduce.7.cloned.1.call-start = ((), (), s32[]{:S(2)}) async-start(), calls=%async_computation.8 | async-start | bytes 28311552 | tf_op jit(solution)/shard_map/psum | solution.py:215
  436.5 14.9 %slice-start.9 = ((s8[6291456]{0:T(1024)(128)(4,1)}), s8[4194304]{0:T(1024)(128)(4,1)S(1)}, s32[]{:S(2)}) async-start(s8[6291456]{0:T(1024)(128)(4,1)} %bitcast.121), calls=%async_computation.18 | async-start | bytes 8388608
  436.5 22.1 %slice-start.11 = ((s8[6291456]{0:T(1024)(128)(4,1)}), s8[4194304]{0:T(1024)(128)(4,1)S(1)}, s32[]{:S(2)}) async-start(s8[6291456]{0:T(1024)(128)(4,1)} %bitcast.123), calls=%async_computation.20 | async-start | bytes 8388608
  441.7 16.9 %slice-start.12 = ((s8[6291456]{0:T(1024)(128)(4,1)}), s8[2097152]{0:T(1024)(128)(4,1)S(1)}, s32[]{:S(2)}) async-start(s8[6291456]{0:T(1024)(128)(4,1)} %bitcast.123), calls=%async_computation.21 | async-start | bytes 4194304
  615.6 225.6 %copy-start.74 = (f32[768]{0:T(1024)}, f32[768]{0:T(1024)S(1)}, u32[]{:S(2)}) copy-start(f32[768]{0:T(1024)S(1)} %get-tuple-element.229) | copy-start | bytes 9220
  (80 other events, 438.5 us)
Sparse Core Ops, SparseCore 0:
  9.6 47.6 all-gather.2
  58.8 44.9 all-gather.4
  331.2 77.0 reduce-scatter.5
  410.5 77.0 reduce-scatter.7
  489.8 77.0 reduce-scatter.3
  573.1 259.6 all-reduce.6
where the time goes:
time: 859 us; the launch traced here: 852 us
  waiting for transfers between devices  325 us (38%)
  matrix products  269 us (31%)
  other arithmetic  116 us (14%)
  blocking collectives  103 us (12%)
  local copies, waits for them, and re-layouts  22.7 us (3%)
  between operations  15.6 us (2%)
    psum x1, waiting for transfers between devices, per_device(): lax.psum((grad_qkv_w, grad_qkv_b, grad_out_w, grad_up_w, grad_up_b, grad_...  217 us
    psum x1, blocking collectives, per_device(): lax.psum((grad_qkv_w, grad_qkv_b, grad_out_w, grad_up_w, grad_up_b, grad_...  61.1 us
    convert_element_type x4, other arithmetic, per_device(): grad_scores = (attn_probs * (grad_probs - weighted)).astype(jnp.bfloat16)  45.4 us
    dot_general x4, matrix products, per_device(): jnp.einsum('qhd,khd->hqk', grad_block, values[:row_stop], preferred_eleme...  42.3 us
    psum x1, blocking collectives, per_device(): lax.psum((vectors[0], vectors[1], vectors[2], vectors[3], vectors[4]), ('...  41.8 us
    all_gather x1, waiting for transfers between devices, per_device(): grad_rows = lax.all_gather(out_grad, 'narrow', axis=0, tiled=True)  41.1 us
    dot_general x4, matrix products, contract_cols(): lax.dot_general(left, right, (((1,), (1,)), ((), ())), preferred_element_...  38.2 us
    all_gather x1, waiting for transfers between devices, per_device(): gathered = lax.all_gather(block_in, 'narrow', axis=0, tiled=True)  37.6 us
  transfers between devices with their start and end apart: 6, of which 4 were waited for; matrix products, arithmetic and copies ran while one was open for 19% of the time, Pallas kernels for 0%

commit v1 on v0

--- a/solution.py
+++ b/solution.py
@@ -95,7 +95,15 @@
     ffn_gain,
     ffn_shift,
 ):
-    gathered = lax.all_gather(block_in, "narrow", axis=0, tiled=True)
+    ways, here, step = (lax.axis_size("narrow"), lax.axis_index("narrow"), block_in.shape[0])
+    line, have = (block_in, 1)
+    while have < ways:
+        line = jnp.concatenate(
+            [line, lax.ppermute(line, "narrow", [(d, (d - have) % ways) for d in range(ways)])],
+            axis=0,
+        )
+        have = 2 * have
+    gathered = jnp.roll(line, here * step, axis=0)
     group_rows = gathered.shape[0]
     local_heads = qkv_weight.shape[1] // (3 * HD)
     segment, place = positions(seq_lens[0], group_rows)

time: 859 us -> 836 us (0.973)
  waiting for transfers between devices: 325 us -> 297 us
    ppermute x0 -> x1, waiting for transfers between devices: none -> 47.8 us  [per_device(): lax.ppermute(line, 'narrow', [(d, (d - have) % ways) for d in range(ways)])]
    all_gather x1, waiting for transfers between devices: 41.1 us -> 0.02 us  [per_device(): grad_rows = lax.all_gather(out_grad, 'narrow', axis=0, tiled=True)]
    all_gather x1 -> x0, waiting for transfers between devices: 37.6 us -> none  [per_device(): gathered = lax.all_gather(block_in, 'narrow', axis=0, tiled=True)]
    unnamed x202 -> x194, local copies, waits for them, and re-layouts: 20.5 us -> 22.4 us
  transfers between devices with their start and end apart: 6 -> 6, of which waited for: 4 -> 3; matrix products, arithmetic and copies ran while one was open for 19% -> 27% of each run, Pallas kernels for 0% -> 0%
where the time goes in v1:
time: 836 us; the launch traced here: 831 us
  waiting for transfers between devices  297 us (36%)
  matrix products  274 us (33%)
  other arithmetic  118 us (14%)
  blocking collectives  99.4 us (12%)
  local copies, waits for them, and re-layouts  24.3 us (3%)
  between operations  15.2 us (2%)
    psum x1, waiting for transfers between devices, per_device(): lax.psum((grad_qkv_w, grad_qkv_b, grad_out_w, grad_up_w, grad_up_b, grad_...  217 us
    psum x1, blocking collectives, per_device(): lax.psum((grad_qkv_w, grad_qkv_b, grad_out_w, grad_up_w, grad_up_b, grad_...  57.6 us
    convert_element_type x4, other arithmetic, per_device(): grad_scores = (attn_probs * (grad_probs - weighted)).astype(jnp.bfloat16)  48.8 us
    ppermute x1, waiting for transfers between devices, per_device(): lax.ppermute(line, 'narrow', [(d, (d - have) % ways) for d in range(ways)])  47.8 us
    psum x1, blocking collectives, per_device(): lax.psum((vectors[0], vectors[1], vectors[2], vectors[3], vectors[4]), ('...  41.8 us
    dot_general x4, matrix products, per_device(): jnp.einsum('qhd,khd->hqk', grad_block, values[:row_stop], preferred_eleme...  41.2 us
    dot_general x4, matrix products, contract_cols(): lax.dot_general(left, right, (((1,), (1,)), ((), ())), preferred_element_...  40.2 us
    dot_general x1, matrix products, per_device(): jnp.dot(second_in, up_weight, preferred_element_type=jnp.float32)  35.9 us
  transfers between devices with their start and end apart: 6, of which 3 were waited for; matrix products, arithmetic and copies ran while one was open for 27% of the time, Pallas kernels for 0%

profile of v1, /device:TPU:0, one launch (start us, length us, event | category | flops | bytes accessed | tf_op | source)
XLA Modules:
  0.0 831.1 jit_solution(14143859187600790800)
XLA Ops:
  21.9 47.8 %collective-permute-done = bf16[1024,768]{1,0:T(8,128)(2,1)} collective-permute-done((bf16[1024,768]{1,0:T(8,128)(2,1)}, bf16[1024,768]{1,0:T(8,128)(2,1)}, u32[]{:S(2)}, u32[]{:S(2)}) %collective-permute-start) | collective-permute-done | bytes 1572896 | tf_op jit(solution)/shard_map/ppermute | solution.py:102
  95.4 8.4 %fusion.146 = (f32[6,512]{1,0:T(8,128)S(1)}, f32[6,512,1536]{2,1,0:T(8,128)}) fusion(bf16[2048,6,64]{0,2,1:T(8,128)(2,1)S(1)} %get-tuple-element.196, bf16[2048,6,64]{0,2,1:T(8,128)(2,1)S(1)} %get-tuple-element.195, pred[512,1536]{1,0:T(8,128)(4,1)S(1)} %copy-done.26), kind=kOutput, calls=%fused_computation.230 | convolution fusion | flops 618132480 | bytes 21245952 | tf_op jit(solution)/shard_map/qhd,khd->hqk/dot_general | solution.py:71
  103.7 9.6 %fusion.2 = f32[6,512]{1,0:T(8,128)} fusion(f32[6,512,1536]{2,1,0:T(8,128)} %get-tuple-element.181, f32[6,512]{1,0:T(8,128)S(1)} %get-tuple-element.180), kind=kLoop, calls=%fused_computation.15 | loop fusion | flops 9434112 | bytes 18898944 | tf_op jit(solution)/shard_map/reduce_sum | solution.py:136
  114.7 11.9 %fusion.145 = (f32[6,512]{1,0:T(8,128)S(1)}, f32[6,512,2048]{2,1,0:T(8,128)}) fusion(bf16[2048,6,48]{0,2,1:T(8,128)(2,1)S(1)} %get-tuple-element.160, bf16[2048,6,8]{0,2,1:T(8,128)(2,1)} %copy-done.24, bf16[2048,6,8]{0,2,1:T(8,128)(2,1)} %copy-done.22, bf16[2048,6,64]{0,2,1:T(8,128)(2,1)} %copy-done.12, pred[512,2048]{1,0:T(8,128)(4,1)} %fusion.35), kind=kOutput, calls=%fused_computation.229 | convolution fusion | flops 828896256 | bytes 28192768 | tf_op jit(solution)/shard_map/qhd,khd->hqk/dot_general | solution.py:71
  126.6 10.9 %fusion = f32[6,512]{1,0:T(8,128)S(1)} fusion(f32[6,512,2048]{2,1,0:T(8,128)} %get-tuple-element.177, f32[6,512]{1,0:T(8,128)S(1)} %get-tuple-element.176), kind=kLoop, calls=%fused_computation.6 | loop fusion | flops 12579840 | bytes 25190400 | tf_op jit(solution)/shard_map/reduce_sum | solution.py:136
  165.2 7.4 multiply_reduce_fusion.2
  186.2 12.5 %multiply_reduce_fusion.1 = (f32[6,512]{1,0:T(8,128)S(1)}, f32[6,512,1536]{2,1,0:T(8,128)}) fusion(f32[6,512,1536]{2,1,0:T(8,128)} %get-tuple-element.181, f32[6,512]{1,0:T(8,128)S(1)} %copy-done.35, bf16[512,6,64]{0,2,1:T(8,128)(2,1)S(1)} %bitcast.116, bf16[2048,6,192]{0,2,1:T(8,128)(2,1)} %copy-done.7), kind=kOutput, calls=%fused_computation.10 | convolution fusion | flops 618132480 | bytes 39346176 | tf_op jit(solution)/shard_map/qhd,khd->hqk/dot_general | solution.py:193
  198.8 8.1 fusion.78
  206.9 14.0 %multiply_convert_fusion.1 = bf16[6,512,1536]{2,1,0:T(8,128)(2,1)S(1)} fusion(f32[6,512,1536]{2,1,0:T(8,128)} %get-tuple-element.183, f32[6,512,1536]{2,1,0:T(8,128)} %get-tuple-element.181, f32[6,512]{1,0:T(8,128)S(1)} %get-tuple-element.182, f32[6,512]{1,0:T(8,128)S(1)} %copy-done.35), kind=kLoop, calls=%fused_computation.9 | loop fusion | flops 18874368 | bytes 47210496 | tf_op jit(solution)/shard_map/convert_element_type | solution.py:197
  227.3 16.3 %multiply_reduce_fusion = (f32[6,512]{1,0:T(8,128)S(1)}, f32[6,512,2048]{2,1,0:T(8,128)}) fusion(f32[6,512,2048]{2,1,0:T(8,128)} %get-tuple-element.177, f32[6,512]{1,0:T(8,128)S(1)} %log_add_fusion, bf16[512,6,64]{0,2,1:T(8,128)(2,1)} %bitcast.114, bf16[2048,6,192]{0,2,1:T(8,128)(2,1)} %copy-done.7), kind=kOutput, calls=%fused_computation.1 | convolution fusion | flops 824177664 | bytes 52322304 | tf_op jit(solution)/shard_map/qhd,khd->hqk/dot_general | solution.py:193
  243.6 21.9 %multiply_convert_fusion = bf16[6,512,2048]{2,1,0:T(8,128)(2,1)} fusion(f32[6,512,2048]{2,1,0:T(8,128)} %get-tuple-element.179, f32[6,512,2048]{2,1,0:T(8,128)} %get-tuple-element.177, f32[6,512]{1,0:T(8,128)S(1)} %get-tuple-element.178, f32[6,512]{1,0:T(8,128)S(1)} %log_add_fusion), kind=kLoop, calls=%fused_computation | loop fusion | flops 25165824 | bytes 62939136 | tf_op jit(solution)/shard_map/convert_element_type | solution.py:197
  265.5 8.7 %fusion.94 = f32[512,6,64]{0,2,1:T(8,128)S(1)} fusion(bf16[6,512,2048]{2,1,0:T(8,128)(2,1)} %multiply_convert_fusion, bf16[2048,6,48]{0,2,1:T(8,128)(2,1)S(1)} %copy-done.11, bf16[2048,6,8]{0,2,1:T(8,128)(2,1)S(1)} %copy-done.25, bf16[2048,6,8]{0,2,1:T(8,128)(2,1)S(1)} %copy-done.23), kind=kOutput, calls=%fused_computation.148 | convolution fusion | flops 810221568 | bytes 14942208 | tf_op jit(solution)/shard_map/hqk,khd->qhd/dot_general | solution.py:199
  286.7 11.8 %fusion.63 = bf16[2048,6,192]{0,2,1:T(8,128)(2,1)} fusion(bf16[2048,6,192]{0,2,1:T(8,128)(2,1)} %slice_dynamic-update-slice_fusion, f32[2048,6,64]{0,2,1:T(8,128)S(1)} %copy-done.6, bf16[512,6,64]{0,2,1:T(8,128)(2,1)S(1)} %bitcast.115, f32[6,512,2048]{2,1,0:T(8,128)} %get-tuple-element.177, f32[6,512]{1,0:T(8,128)S(1)} %log_add_fusion), kind=kOutput, calls=%fused_computation.111 | convolution fusion | flops 818675712 | bytes 31862784 | tf_op jit(solution)/shard_map/hqk,qhd->khd/dot_general | solution.py:186
  298.5 9.8 %fusion.150 = f32[2048,768]{1,0:T(8,128)} fusion(bf16[2048,1152]{0,1:T(8,128)(2,1)} %bitcast.26, bf16[768,1152]{1,0:T(8,128)(2,1)} %param.38), kind=kOutput, calls=%fused_computation.234 | convolution fusion | flops 3623878656 | bytes 12779520 | tf_op jit(solution)/shard_map/dot_general | solution.py:62
  309.1 35.9 %multiply_convert_fusion.3 = (bf16[2048,1536]{1,0:T(8,128)(2,1)}, f32[2048,1536]{1,0:T(8,128)}, f32[2048,1536]{1,0:T(8,128)}) fusion(f32[1536]{0:T(1024)S(1)} %convert_element_type.145, bf16[768,1536]{1,0:T(8,128)(2,1)S(1)} %copy-done, bf16[2048,768]{1,0:T(8,128)(2,1)} %copy-done.14, f32[768]{0:T(1024)S(1)} %convert_element_type.143, ...), kind=kOutput, calls=%fused_computation.25 | convolution fusion | flops 5048893440 | bytes 36990976 | tf_op jit(solution)/shard_map/dot_general | solution.py:124
  345.1 17.1 %convert_reduce_fusion = (f32[1536]{0:T(1024)S(1)}, bf16[2048,1536]{1,0:T(8,128)(2,1)}) fusion(f32[2048,1536]{1,0:T(8,128)} %get-tuple-element.153, bf16[2048,768]{1,0:T(8,128)(2,1)S(1)} %copy-done.71, bf16[1536,768]{1,0:T(8,128)(2,1)S(1)} %copy-done.73, f32[2048,1536]{1,0:T(8,128)} %get-tuple-element.192, f32[1536]{0:T(1024)S(1)} %convert_element_type.145), kind=kOutput, calls=%fused_computation.19 | convolution fusion | flops 4885314048 | bytes 36974592 | tf_op jit(solution)/shard_map/dot_general | solution.py:62
  362.2 9.8 %fusion.151 = f32[2048,768]{1,0:T(8,128)} fusion(bf16[2048,1536]{1,0:T(8,128)(2,1)} %get-tuple-element.194, bf16[768,1536]{1,0:T(8,128)(2,1)S(1)} %copy-done), kind=kOutput, calls=%fused_computation.235 | convolution fusion | flops 4831838208 | bytes 14942208 | tf_op jit(solution)/shard_map/dot_general | solution.py:62
  390.8 12.2 %fusion.104 = bf16[512,6,64]{0,2,1:T(8,128)(2,1)S(1)} fusion(f32[6,512,2048]{2,1,0:T(8,128)} %get-tuple-element.177, f32[6,512]{1,0:T(8,128)S(1)} %copy-done.52, f32[6,512]{1,0:T(8,128)S(1)} %copy-done.50, bf16[2048,6,192]{0,2,1:T(8,128)(2,1)} %copy-done.7), kind=kOutput, calls=%fused_computation.159 | convolution fusion | flops 824377344 | bytes 27156480 | tf_op jit(solution)/shard_map/hqk,khd->qhd/dot_general | solution.py:140
  403.2 7.7 fusion.149
  420.8 9.7 %fusion.137 = f32[768,1152]{1,0:T(8,128)} fusion(bf16[2048,1152]{0,1:T(8,128)(2,1)} %bitcast.26, bf16[2048,768]{1,0:T(8,128)(2,1)S(1)} %copy-done.15, f32[768]{0:T(1024)S(1)} %copy-done.63, f32[768]{0:T(1024)S(1)} %copy-done.54, f32[2048]{0:T(1024)S(1)} %copy-done.60, f32[2048]{0:T(1024)S(1)} %copy-done.58), kind=kOutput, calls=%fused_computation.225 | convolution fusion | flops 3633315840 | bytes 11425792 | tf_op jit(solution)/shard_map/dot_general | solution.py:56
  452.6 57.6 %all-reduce.3 = (f32[1152]{0:T(1024)}, f32[1536]{0:T(1024)}) all-reduce(f32[1152]{0:T(1024)S(1)} %reduce_sum.246, f32[1536]{0:T(1024)S(1)} %get-tuple-element.193), channel_id=1, replica_groups=mesh['wide'=16,'narrow'=2] {'wide'}, use_global_device_ids=true, to_apply=%region_28.29 | all-reduce | flops 2688 | bytes 21504 | tf_op jit(solution)/shard_map/psum | solution.py:223
  515.0 31.7 %reduce-scatter.4.cloned.1.call-done = f32[1024,768]{1,0:T(8,128)} async-done(((f32[2048,768]{1,0:T(8,128)}), f32[1024,768]{1,0:T(8,128)}) %reduce-scatter.4.cloned.1.call-update) | async-done | bytes 3145744 | tf_op jit(solution)/shard_map/reduce_scatter | solution.py:155
  553.6 41.8 %all-reduce.2 = (f32[768]{0:T(1024)S(1)}, f32[768]{0:T(1024)}, f32[768]{0:T(1024)}, f32[768]{0:T(1024)}, f32[768]{0:T(1024)}) all-reduce(f32[768]{0:T(1024)S(1)} %get-tuple-element.162, f32[768]{0:T(1024)S(1)} %get-tuple-element.128, f32[768]{0:T(1024)S(1)} %get-tuple-element.133, ...), channel_id=1, replica_groups=mesh['wide'=16,'narrow'=2] {'wide','narrow'}, use_global_device_ids=true, to_apply=%region_31.32 | all-reduce | flops 3840 | bytes 30720 | tf_op jit(solution)/shard_map/psum | solution.py:243
  595.4 217.2 %all-reduce.7.cloned.1.call-done = (f32[768,1152]{1,0:T(8,128)}, f32[384,768]{1,0:T(8,128)}, f32[768,1536]{1,0:T(8,128)}, f32[1536,768]{1,0:T(8,128)}) async-done(((f32[768,1152]{1,0:T(8,128)}, f32[384,768]{1,0:T(8,128)}, f32[768,1536]{1,0:T(8,128)}, f32[1536,768]{1,0:T(8,128)}), (f32[768,1152]{1,0:T(8,128)}, f32[384,768]{1,0:T(8,128)}, f32[768,1536]{1,0:T(8,128)}, ...) | async-done | bytes 14155792 | tf_op jit(solution)/shard_map/psum | solution.py:223
  (297 shorter events, 176.2 us)
Async XLA Ops:
  7.2 301.9 %copy-start = (bf16[768,1536]{1,0:T(8,128)(2,1)S(1)}, bf16[768,1536]{1,0:T(8,128)(2,1)}, u32[]{:S(2)}) copy-start(bf16[768,1536]{1,0:T(8,128)(2,1)} %param.42) | copy-start | bytes 7077892
  7.2 130.4 %all-gather.2.cloned.1.call-start = ((), (), s32[]{:S(2)}) async-start(), calls=%async_computation.4 | async-start | bytes 4718592 | tf_op jit(solution)/shard_map/all_gather | solution.py:162
  7.9 502.3 %reduce-scatter.6.cloned.1.call-start = ((), (), s32[]{:S(2)}) async-start(), calls=%async_computation.5 | async-start | bytes 9437184 | tf_op jit(solution)/shard_map/reduce_scatter | solution.py:227
  8.0 61.7 %collective-permute-start = (bf16[1024,768]{1,0:T(8,128)(2,1)}, bf16[1024,768]{1,0:T(8,128)(2,1)}, u32[]{:S(2)}, u32[]{:S(2)}) collective-permute-start(bf16[1024,768]{1,0:T(8,128)(2,1)} %param.35), channel_id=1, source_target_pairs={{0,1},{1,0},{2,3},{3,2},{4,5},{5,4},{6,7},{7,6},{8,9},{9,8},{10,11... | collective-permute-start | bytes 4718600 | tf_op jit(solution)/shard_map/ppermute | solution.py:102
  13.3 67.1 %copy-start.53 = (f32[768]{0:T(1024)}, f32[768]{0:T(1024)S(1)}, u32[]{:S(2)}) copy-start(f32[768]{0:T(1024)S(1)} %convert_element_type.131) | copy-start | bytes 9220
  14.0 66.5 %copy-start.62 = (f32[768]{0:T(1024)}, f32[768]{0:T(1024)S(1)}, u32[]{:S(2)}) copy-start(f32[768]{0:T(1024)S(1)} %convert_element_type.132) | copy-start | bytes 9220
  15.7 60.0 %copy-start.75 = (bf16[768,1152]{1,0:T(8,128)(2,1)S(1)}, bf16[768,1152]{1,0:T(8,128)(2,1)}, u32[]{:S(2)}) copy-start(bf16[768,1152]{1,0:T(8,128)(2,1)} %param.38) | copy-start | bytes 5308420
  18.0 63.4 %copy-start.27 = (f32[2048,8]{0,1:T(8,128)}, f32[2048,8]{0,1:T(8,128)S(1)}, u32[]{:S(2)}) copy-start(f32[2048,8]{0,1:T(8,128)S(1)} %get-tuple-element.171) | copy-start | bytes 196612
  81.5 33.2 %copy-start.10 = (bf16[2048,6,48]{0,2,1:T(8,128)(2,1)}, bf16[2048,6,48]{0,2,1:T(8,128)(2,1)S(1)}, u32[]{:S(2)}) copy-start(bf16[2048,6,48]{0,2,1:T(8,128)(2,1)S(1)} %get-tuple-element.160) | copy-start | bytes 3538948
  206.9 14.0 %copy-start.5 = (f32[2048,6,64]{0,2,1:T(8,128)}, f32[2048,6,64]{0,2,1:T(8,128)S(1)}, u32[]{:S(2)}) copy-start(f32[2048,6,64]{0,2,1:T(8,128)S(1)} %fusion.78) | copy-start | bytes 9437188
  243.6 21.9 %copy-start.11 = (bf16[2048,6,48]{0,2,1:T(8,128)(2,1)S(1)}, bf16[2048,6,48]{0,2,1:T(8,128)(2,1)}, u32[]{:S(2)}) copy-start(bf16[2048,6,48]{0,2,1:T(8,128)(2,1)} %copy-done.10) | copy-start | bytes 3538948
  243.6 21.9 %copy-start.23 = (bf16[2048,6,8]{0,2,1:T(8,128)(2,1)S(1)}, bf16[2048,6,8]{0,2,1:T(8,128)(2,1)}, u32[]{:S(2)}) copy-start(bf16[2048,6,8]{0,2,1:T(8,128)(2,1)} %copy-done.22) | copy-start | bytes 589828
  243.6 21.9 %copy-start.25 = (bf16[2048,6,8]{0,2,1:T(8,128)(2,1)S(1)}, bf16[2048,6,8]{0,2,1:T(8,128)(2,1)}, u32[]{:S(2)}) copy-start(bf16[2048,6,8]{0,2,1:T(8,128)(2,1)} %copy-done.24) | copy-start | bytes 589828
  308.4 201.8 %reduce-scatter.8.cloned.1.call-start = ((), (), s32[]{:S(2)}) async-start(), calls=%async_computation.6 | async-start | bytes 9437184 | tf_op jit(solution)/shard_map/reduce_scatter | solution.py:228
  309.1 36.0 %copy-start.55 = (f32[768]{0:T(1024)}, f32[768]{0:T(1024)S(1)}, u32[]{:S(2)}) copy-start(f32[768]{0:T(1024)S(1)} %convert_element_type.142) | copy-start | bytes 9220
  309.1 36.0 %copy-start.64 = (f32[768]{0:T(1024)}, f32[768]{0:T(1024)S(1)}, u32[]{:S(2)}) copy-start(f32[768]{0:T(1024)S(1)} %convert_element_type.143) | copy-start | bytes 9220
  309.1 35.9 %copy-start.71 = (bf16[2048,768]{1,0:T(8,128)(2,1)S(1)}, bf16[2048,768]{1,0:T(8,128)(2,1)}, u32[]{:S(2)}) copy-start(bf16[2048,768]{1,0:T(8,128)(2,1)} %all-gather.2.cloned.1.call-done) | copy-start | bytes 9437188
  309.1 35.9 %copy-start.73 = (bf16[1536,768]{1,0:T(8,128)(2,1)S(1)}, bf16[1536,768]{1,0:T(8,128)(2,1)}, u32[]{:S(2)}) copy-start(bf16[1536,768]{1,0:T(8,128)(2,1)} %param.44) | copy-start | bytes 7077892
  372.0 174.7 %reduce-scatter.4.cloned.1.call-start = ((), (), s32[]{:S(2)}) async-start(), calls=%async_computation.3 | async-start | bytes 9437184 | tf_op jit(solution)/shard_map/reduce_scatter | solution.py:155
  415.4 397.2 %all-reduce.7.cloned.1.call-start = ((), (), s32[]{:S(2)}) async-start(), calls=%async_computation.7 | async-start | bytes 28311552 | tf_op jit(solution)/shard_map/psum | solution.py:223
  415.5 15.0 %slice-start.14 = ((s8[6291456]{0:T(1024)(128)(4,1)}), s8[4194304]{0:T(1024)(128)(4,1)S(1)}, s32[]{:S(2)}) async-start(s8[6291456]{0:T(1024)(128)(4,1)} %bitcast.125), calls=%async_computation.22 | async-start | bytes 8388608
  415.5 22.2 %slice-start.16 = ((s8[6291456]{0:T(1024)(128)(4,1)}), s8[4194304]{0:T(1024)(128)(4,1)S(1)}, s32[]{:S(2)}) async-start(s8[6291456]{0:T(1024)(128)(4,1)} %bitcast.127), calls=%async_computation.24 | async-start | bytes 8388608
  420.8 16.9 %slice-start.17 = ((s8[6291456]{0:T(1024)(128)(4,1)}), s8[2097152]{0:T(1024)(128)(4,1)S(1)}, s32[]{:S(2)}) async-start(s8[6291456]{0:T(1024)(128)(4,1)} %bitcast.127), calls=%async_computation.25 | async-start | bytes 4194304
  595.4 225.6 %copy-start.66 = (f32[768]{0:T(1024)}, f32[768]{0:T(1024)S(1)}, u32[]{:S(2)}) copy-start(f32[768]{0:T(1024)S(1)} %get-tuple-element.231) | copy-start | bytes 9220
  (76 other events, 433.4 us)
Sparse Core Ops, SparseCore 0:
  9.6 69.9 all-gather.1
  308.5 79.3 reduce-scatter.5
  390.4 77.0 reduce-scatter.7
  469.6 77.0 reduce-scatter.3
  552.9 259.6 all-reduce.6
